TPU v7x, 256 devices: a whole 4x4x8 slice. The times are simulated.
256 devices in a mesh: fibre: 2 (over core), chan: 128 (over z, x, y).
Axes of the slice: x: 4, y: 4, z: 8, core: 2. Of those that a mesh axis runs over, the one named last changes fastest.
Arguments:
- raw: bfloat16 [32768, 4096], P(('fibre', 'chan'))
- starts: int32 [4], replicated, may hold values from 0 to 3072, as said below
- ref_ids: int32 [64], replicated, may hold values from 0 to 32767, as said below
- near_ids: int32 [32768, 8], P(('fibre', 'chan')), may hold values from 0 to 32767, as said below
- cross_ids: int32 [32768, 2], P(('fibre', 'chan')), may hold values from 0 to 255
- cross_mask: int32 [32768, 2], P(('fibre', 'chan')), may hold values 0 or 1
- export_loc: int32 [256], P(('fibre', 'chan')), may hold values from 0 to 127
Outputs:
- correlations: bfloat16 [32768, 64, 512], P(('fibre', 'chan'))
Inputs may be any that keep to these rules, and one draw needn't show every extreme that they name: starts[3] is 3072. `ref_ids`: distinct channel ids. `near_ids`: each neighbour lies on the same route as its channel (route = id // 16384) and at most 16 channels away from it.
All inputs are finite; a program needn't handle non-finite values. No bound on the sum of `cross_mask` on one device may be relied on, other than what follows from the above.
Results may differ from a plain program's by a relative error of at most 0.0063.
The roundings to bfloat16 on the way count: a program that leaves them out, or rounds other values in their place, can miss the bound.
Values may be sent and summed in bfloat16 or wider, within the bound.
A program may use at most 128 MiB of HBM per device.

v0:
```python
import math
import jax
import jax.numpy as jnp
from jax import lax
from jax.sharding import PartitionSpec as P

SEG = 1024
SEGS = 4
REFS = 64
LAGS = 512
NN = 8
HALO = 16


def with_halo(block, sides, width):
    for axis, dim in sides:
        count = lax.axis_size(axis)
        forward = [(i, i + 1) for i in range(count - 1)]
        backward = [(target, source) for source, target in forward]
        low = lax.ppermute(
            lax.slice_in_dim(block, block.shape[dim] - width, None, axis=dim), axis, forward
        )
        high = lax.ppermute(lax.slice_in_dim(block, 0, width, axis=dim), axis, backward)
        block = jnp.concatenate([low, block, high], axis=dim)
    return block


def forward_table():
    nbins = SEG // 2
    sample = jnp.arange(SEG, dtype=jnp.int32)
    freq = jnp.arange(nbins, dtype=jnp.int32)
    phase = jnp.mod(sample[:, None] * freq[None, :], SEG).astype(jnp.float32)
    theta = phase * (2.0 * math.pi / SEG)
    keep = (freq > 0).astype(jnp.float32)[None, :]
    return jnp.concatenate([jnp.cos(theta) * keep, -jnp.sin(theta)], 1).astype(jnp.bfloat16)


def lag_table():
    nbins = SEG // 2
    freq = jnp.arange(nbins, dtype=jnp.int32)
    lag = jnp.arange(LAGS, dtype=jnp.int32) - LAGS // 2
    phase = jnp.mod(freq[:, None] * lag[None, :], SEG).astype(jnp.float32)
    theta = phase * (2.0 * math.pi / SEG)
    scale = 1.0 / math.sqrt(nbins)
    table = jnp.concatenate([jnp.cos(theta) * scale, -jnp.sin(theta) * scale], 0)
    return table.astype(jnp.bfloat16)


def per_device(raw, starts, ref_ids, near_ids, cross_ids, cross_mask, export_loc):
    nbins = SEG // 2
    width = SEGS * SEG
    local_ch = raw.shape[0]
    block_base = lax.axis_index(("fibre", "chan")) * local_ch
    pieces = [lax.dynamic_slice_in_dim(raw, starts[s], SEG, 1) for s in range(SEGS)]
    segment = jnp.stack(pieces, 1)
    spectrum = jnp.dot(
        segment.reshape(local_ch * SEGS, SEG), forward_table(), preferred_element_type=jnp.float32
    )
    power = jnp.sum(spectrum * spectrum, -1, keepdims=True) / nbins
    whitened = (spectrum / jnp.sqrt(power + 1e-06)).astype(jnp.bfloat16)
    flat = whitened.reshape(local_ch, width)
    columns = jnp.arange(local_ch, dtype=jnp.int32)
    pick = (ref_ids[:, None] - block_base == columns[None, :]).astype(jnp.bfloat16)
    selected = jnp.dot(pick, flat, preferred_element_type=jnp.float32)
    references = lax.psum(selected, ("fibre", "chan")).astype(jnp.bfloat16)
    extended = with_halo(flat, (("chan", 0),), HALO)
    ext_rows = local_ch + 2 * HALO
    position = near_ids - (block_base - HALO)
    near_count = jnp.sum(
        (position[:, :, None] == jnp.arange(ext_rows, dtype=jnp.int32)[None, None, :]).astype(
            jnp.float32
        ),
        1,
    )
    total = flat.astype(jnp.float32) + jnp.dot(
        near_count.astype(jnp.bfloat16), extended, preferred_element_type=jnp.float32
    )
    exported = jnp.take(flat, export_loc, axis=0)
    live = cross_mask == 1
    piece = lax.all_gather(exported, ("fibre", "chan"), axis=0, tiled=True)
    slots = jnp.arange(piece.shape[0], dtype=jnp.int32)
    hits = (cross_ids[:, :, None] == slots[None, None, :]) & live[:, :, None]
    weights = jnp.sum(hits.astype(jnp.float32), 1).astype(jnp.bfloat16)
    crossing = jnp.dot(weights, piece, preferred_element_type=jnp.float32)
    count = 1.0 + NN + jnp.sum(cross_mask.astype(jnp.float32), 1)
    smoothed = ((total + crossing) / count[:, None]).astype(jnp.bfloat16)
    kernel = lag_table()
    ref_split = references.reshape(REFS, SEGS, SEG)
    ref_re = ref_split[..., :nbins]
    ref_im = ref_split[..., nbins:]
    group = math.gcd(local_ch, 32)

    def correlate(rows):
        a_re = rows[..., :nbins]
        a_im = rows[..., nbins:]
        g_re = jnp.einsum(
            "csf,rsf->crf", a_re, ref_re, preferred_element_type=jnp.float32
        ) + jnp.einsum("csf,rsf->crf", a_im, ref_im, preferred_element_type=jnp.float32)
        g_im = jnp.einsum(
            "csf,rsf->crf", a_im, ref_re, preferred_element_type=jnp.float32
        ) - jnp.einsum("csf,rsf->crf", a_re, ref_im, preferred_element_type=jnp.float32)
        cross = (jnp.concatenate([g_re, g_im], -1) / SEGS).astype(jnp.bfloat16)
        out = jnp.dot(cross.reshape(group * REFS, SEG), kernel, preferred_element_type=jnp.float32)
        return out.astype(jnp.bfloat16).reshape(group, REFS, LAGS)

    result = lax.map(correlate, smoothed.reshape(local_ch // group, group, SEGS, SEG))
    return result.reshape(local_ch, REFS, LAGS)


def solution(mesh):
    in_specs = (
        P(("fibre", "chan"), None),
        P(),
        P(),
        P(("fibre", "chan"), None),
        P(("fibre", "chan"), None),
        P(("fibre", "chan"), None),
        P(("fibre", "chan")),
    )
    out_specs = P(("fibre", "chan"), None, None)
    return jax.shard_map(
        per_device, mesh=mesh, in_specs=in_specs, out_specs=out_specs, check_vma=False
    )
```

profile of v0, /device:TPU:1, one launch (start us, length us, event | category | flops | bytes accessed | tf_op | source)
XLA Modules:
  0.0 315.5 jit_solution(655089644088672558)
XLA Ops:
  6.5 1.5 fusion.53
  13.1 8.0 %negate_convert_fusion = bf16[1024,512]{1,0:T(8,128)(2,1)S(1)} fusion(), kind=kLoop, calls=%fused_computation.36 | loop fusion | flops 8388608 | bytes 1048576 | tf_op jit(solution)/shard_map/convert.3
  23.6 1.9 dynamic-slice_bitcast_fusion.3
  25.6 0.8 copy.42
  26.4 0.3 reshape.58
  26.7 7.9 %multiply_convert_fusion = bf16[1024,512]{1,0:T(8,128)(2,1)S(1)} fusion(f32[512]{0:T(512)S(1)} %fusion.48), kind=kLoop, calls=%fused_computation.37 | loop fusion | flops 8388608 | bytes 1050624 | tf_op jit(solution)/shard_map/convert.2
  34.7 1.3 multiply_reduce_fusion
  36.0 0.3 divide_convert_fusion
  36.3 0.7 reshape.59
  37.7 0.6 fusion.46
  38.5 4.0 %collective-permute-start = (bf16[16,4096]{1,0:T(8,128)(2,1)S(1)}, bf16[16,4096]{1,0:T(8,128)(2,1)S(1)}, u32[]{:S(2)}, u32[]{:S(2)}) collective-permute-start(bf16[16,4096]{1,0:T(8,128)(2,1)S(1)} %slice.41), channel_id=1, source_target_pairs={{0,1},{1,2},{2,3},{3,4},{4,5},{5,6},{6,7},{7,8},{8,9},{9,10},{10,1... | collective-permute-start | bytes 393224 | tf_op jit(solution)/shard_map/ppermute | solution.py:20
  42.6 1.3 collective-permute-start.1
  43.9 0.3 fusion.45
  44.3 88.9 %all-reduce.1 = bf16[64,4096]{1,0:T(8,128)(2,1)S(1)} all-reduce(f32[64,4096]{1,0:T(8,128)S(1)} %fusion.45), channel_id=1, replica_groups=mesh['fibre'=2,'chan'=128] {'fibre','chan'}, use_global_device_ids=true, to_apply=%region_4.5 | all-reduce | flops 262144 | bytes 1572864 | tf_op jit(solution)/shard_map/psum | solution.py:65
  133.2 0.4 reshape.61
  133.8 1.1 copy.48
  134.9 1.1 copy.49
  136.3 4.5 %multiply_convert_fusion.2 = (bf16[512,512]{1,0:T(8,128)(2,1)S(1)}, bf16[512,512]{1,0:T(8,128)(2,1)S(1)}) fusion(s32[512]{0:T(512)S(1)} %iota_add_fusion), kind=kLoop, calls=%fused_computation.55 | loop fusion | flops 4980736 | bytes 1050624 | tf_op jit(solution)/shard_map/convert
  140.8 1.0 pad_maximum_fusion.1
  141.9 16.6 %all-gather.3.cloned.1.call-done = bf16[256,1,4096]{2,1,0:T(2,128)(2,1)} async-done(((bf16[1,1,4096]{2,1,0:T(2,128)(2,1)}), bf16[256,1,4096]{2,1,0:T(2,128)(2,1)}) %all-gather.3.cloned.1.call-update) | async-done | bytes 2097168 | tf_op jit(solution)/shard_map/all_gather | solution.py:80
  158.5 4.7 %fusion.25 = f32[128,4096]{1,0:T(8,128)S(1)} fusion(bf16[256,1,4096]{2,1,0:T(2,128)(2,1)} %all-gather.3.cloned.1.call-done, bf16[128,256]{1,0:T(8,128)(2,1)S(1)} %convert_reduce_fusion.1), kind=kOutput, calls=%fused_computation.31 | convolution fusion | flops 268435456 | bytes 4259840 | tf_op jit(solution)/shard_map/dot_general | solution.py:84
  163.2 0.6 fusion.17
  163.8 0.8 reshape.60
  164.9 143.8 %while.11 = (s32[]{:T(128)}, bf16[4,32,64,512]{3,2,1,0:T(8,128)(2,1)}, bf16[4,32,4,1024]{3,2,1,0:T(4,128)(2,1)S(1)}, bf16[64,4,512]{0,1,2:T(4,128)(2,1)S(1)}, bf...) while((s32[]{:T(128)}, ...), condition=%wide.region_6.7_spmd, body=%wide.region_5.6_spmd.sunk | while | flops 2190475264 | bytes 77595424 | solution.py:106
  164.9 1.0 copy-done
  166.0 0.8 copy.57
  166.8 1.3 fusion.87
  168.1 4.9 %add_bitcast_fusion.2 = f32[32,64,512]{1,0,2:T(8,128)} fusion(f32[512,32,64]{2,1,0:T(8,128)S(1)} %fusion.87, bf16[64,4,512]{0,1,2:T(4,128)(2,1)S(1)} %copy-done.6, bf16[1,32,4,1024]{1,2,3,0:T(4,128)(2,1)S(1)} %copy.57), kind=kOutput, calls=%fused_computation.3.clone.1 | convolution fusion | flops 9437184 | bytes 8912896 | tf_op jit(solution)/shard_map/while/body/eval_jaxpr/csf,rsf->crf/dot_general | solution.py:98
  173.1 6.9 %copy.59 = f32[32,64,512]{2,1,0:T(8,128)} copy(f32[32,64,512]{1,0,2:T(8,128)} %add_bitcast_fusion.2) | data formatting | bytes 8388608 | tf_op jit(solution)/shard_map/while/body/eval_jaxpr/add | solution.py:96
  180.0 1.3 fusion.86
  181.3 4.9 %subtract_bitcast_fusion.2 = f32[32,64,512]{1,0,2:T(8,128)} fusion(f32[512,32,64]{2,1,0:T(8,128)S(1)} %fusion.86, bf16[64,4,512]{0,1,2:T(4,128)(2,1)S(1)} %copy-done.7, bf16[1,32,4,1024]{1,2,3,0:T(4,128)(2,1)S(1)} %copy.57), kind=kOutput, calls=%fused_computation.2.clone.1 | convolution fusion | flops 9437184 | bytes 8912896 | tf_op jit(solution)/shard_map/while/body/eval_jaxpr/csf,rsf->crf/dot_general | solution.py:101
  186.2 6.9 %copy.58 = f32[32,64,512]{2,1,0:T(8,128)} copy(f32[32,64,512]{1,0,2:T(8,128)} %subtract_bitcast_fusion.2) | data formatting | bytes 8388608 | tf_op jit(solution)/shard_map/while/body/eval_jaxpr/sub | solution.py:99
  193.2 5.8 %fusion.88 = bf16[2048,512]{1,0:T(8,128)(2,1)S(1)} fusion(bf16[1024,512]{1,0:T(8,128)(2,1)S(1)} %copy-done.2, f32[2048,512]{1,0:T(8,128)} %bitcast.74, f32[2048,512]{1,0:T(8,128)} %bitcast.73), kind=kOutput, calls=%fused_computation.6.clone.1 | convolution fusion | flops 2154823680 | bytes 11534336 | tf_op jit(solution)/shard_map/while/body/eval_jaxpr/dot_general | solution.py:103
  199.0 1.6 constant_dynamic-update-slice_fusion.2
  200.8 1.0 copy-done
  202.0 0.8 copy.57
  202.7 1.3 fusion.87
  204.1 4.9 %add_bitcast_fusion.2 = f32[32,64,512]{1,0,2:T(8,128)} fusion(f32[512,32,64]{2,1,0:T(8,128)S(1)} %fusion.87, bf16[64,4,512]{0,1,2:T(4,128)(2,1)S(1)} %copy-done.6, bf16[1,32,4,1024]{1,2,3,0:T(4,128)(2,1)S(1)} %copy.57), kind=kOutput, calls=%fused_computation.3.clone.1 | convolution fusion | flops 9437184 | bytes 8912896 | tf_op jit(solution)/shard_map/while/body/eval_jaxpr/csf,rsf->crf/dot_general | solution.py:98
  209.0 6.9 %copy.59 = f32[32,64,512]{2,1,0:T(8,128)} copy(f32[32,64,512]{1,0,2:T(8,128)} %add_bitcast_fusion.2) | data formatting | bytes 8388608 | tf_op jit(solution)/shard_map/while/body/eval_jaxpr/add | solution.py:96
  215.9 1.3 fusion.86
  217.2 4.9 %subtract_bitcast_fusion.2 = f32[32,64,512]{1,0,2:T(8,128)} fusion(f32[512,32,64]{2,1,0:T(8,128)S(1)} %fusion.86, bf16[64,4,512]{0,1,2:T(4,128)(2,1)S(1)} %copy-done.7, bf16[1,32,4,1024]{1,2,3,0:T(4,128)(2,1)S(1)} %copy.57), kind=kOutput, calls=%fused_computation.2.clone.1 | convolution fusion | flops 9437184 | bytes 8912896 | tf_op jit(solution)/shard_map/while/body/eval_jaxpr/csf,rsf->crf/dot_general | solution.py:101
  222.2 6.9 %copy.58 = f32[32,64,512]{2,1,0:T(8,128)} copy(f32[32,64,512]{1,0,2:T(8,128)} %subtract_bitcast_fusion.2) | data formatting | bytes 8388608 | tf_op jit(solution)/shard_map/while/body/eval_jaxpr/sub | solution.py:99
  229.1 5.8 %fusion.88 = bf16[2048,512]{1,0:T(8,128)(2,1)S(1)} fusion(bf16[1024,512]{1,0:T(8,128)(2,1)S(1)} %copy-done.2, f32[2048,512]{1,0:T(8,128)} %bitcast.74, f32[2048,512]{1,0:T(8,128)} %bitcast.73), kind=kOutput, calls=%fused_computation.6.clone.1 | convolution fusion | flops 2154823680 | bytes 11534336 | tf_op jit(solution)/shard_map/while/body/eval_jaxpr/dot_general | solution.py:103
  235.0 1.6 constant_dynamic-update-slice_fusion.2
  236.8 1.0 copy-done
  237.9 0.8 copy.57
  238.7 1.3 fusion.87
  240.0 4.9 %add_bitcast_fusion.2 = f32[32,64,512]{1,0,2:T(8,128)} fusion(f32[512,32,64]{2,1,0:T(8,128)S(1)} %fusion.87, bf16[64,4,512]{0,1,2:T(4,128)(2,1)S(1)} %copy-done.6, bf16[1,32,4,1024]{1,2,3,0:T(4,128)(2,1)S(1)} %copy.57), kind=kOutput, calls=%fused_computation.3.clone.1 | convolution fusion | flops 9437184 | bytes 8912896 | tf_op jit(solution)/shard_map/while/body/eval_jaxpr/csf,rsf->crf/dot_general | solution.py:98
  245.0 6.9 %copy.59 = f32[32,64,512]{2,1,0:T(8,128)} copy(f32[32,64,512]{1,0,2:T(8,128)} %add_bitcast_fusion.2) | data formatting | bytes 8388608 | tf_op jit(solution)/shard_map/while/body/eval_jaxpr/add | solution.py:96
  251.9 1.3 fusion.86
  253.2 4.9 %subtract_bitcast_fusion.2 = f32[32,64,512]{1,0,2:T(8,128)} fusion(f32[512,32,64]{2,1,0:T(8,128)S(1)} %fusion.86, bf16[64,4,512]{0,1,2:T(4,128)(2,1)S(1)} %copy-done.7, bf16[1,32,4,1024]{1,2,3,0:T(4,128)(2,1)S(1)} %copy.57), kind=kOutput, calls=%fused_computation.2.clone.1 | convolution fusion | flops 9437184 | bytes 8912896 | tf_op jit(solution)/shard_map/while/body/eval_jaxpr/csf,rsf->crf/dot_general | solution.py:101
  258.1 6.9 %copy.58 = f32[32,64,512]{2,1,0:T(8,128)} copy(f32[32,64,512]{1,0,2:T(8,128)} %subtract_bitcast_fusion.2) | data formatting | bytes 8388608 | tf_op jit(solution)/shard_map/while/body/eval_jaxpr/sub | solution.py:99
  265.1 5.8 %fusion.88 = bf16[2048,512]{1,0:T(8,128)(2,1)S(1)} fusion(bf16[1024,512]{1,0:T(8,128)(2,1)S(1)} %copy-done.2, f32[2048,512]{1,0:T(8,128)} %bitcast.74, f32[2048,512]{1,0:T(8,128)} %bitcast.73), kind=kOutput, calls=%fused_computation.6.clone.1 | convolution fusion | flops 2154823680 | bytes 11534336 | tf_op jit(solution)/shard_map/while/body/eval_jaxpr/dot_general | solution.py:103
  270.9 1.6 constant_dynamic-update-slice_fusion.2
  272.7 1.0 copy-done
  273.9 0.8 copy.57
  274.6 1.3 fusion.87
  276.0 4.9 %add_bitcast_fusion.2 = f32[32,64,512]{1,0,2:T(8,128)} fusion(f32[512,32,64]{2,1,0:T(8,128)S(1)} %fusion.87, bf16[64,4,512]{0,1,2:T(4,128)(2,1)S(1)} %copy-done.6, bf16[1,32,4,1024]{1,2,3,0:T(4,128)(2,1)S(1)} %copy.57), kind=kOutput, calls=%fused_computation.3.clone.1 | convolution fusion | flops 9437184 | bytes 8912896 | tf_op jit(solution)/shard_map/while/body/eval_jaxpr/csf,rsf->crf/dot_general | solution.py:98
  280.9 6.9 %copy.59 = f32[32,64,512]{2,1,0:T(8,128)} copy(f32[32,64,512]{1,0,2:T(8,128)} %add_bitcast_fusion.2) | data formatting | bytes 8388608 | tf_op jit(solution)/shard_map/while/body/eval_jaxpr/add | solution.py:96
  287.8 1.3 fusion.86
  289.1 4.9 %subtract_bitcast_fusion.2 = f32[32,64,512]{1,0,2:T(8,128)} fusion(f32[512,32,64]{2,1,0:T(8,128)S(1)} %fusion.86, bf16[64,4,512]{0,1,2:T(4,128)(2,1)S(1)} %copy-done.7, bf16[1,32,4,1024]{1,2,3,0:T(4,128)(2,1)S(1)} %copy.57), kind=kOutput, calls=%fused_computation.2.clone.1 | convolution fusion | flops 9437184 | bytes 8912896 | tf_op jit(solution)/shard_map/while/body/eval_jaxpr/csf,rsf->crf/dot_general | solution.py:101
  294.1 6.9 %copy.58 = f32[32,64,512]{2,1,0:T(8,128)} copy(f32[32,64,512]{1,0,2:T(8,128)} %subtract_bitcast_fusion.2) | data formatting | bytes 8388608 | tf_op jit(solution)/shard_map/while/body/eval_jaxpr/sub | solution.py:99
  301.0 5.8 %fusion.88 = bf16[2048,512]{1,0:T(8,128)(2,1)S(1)} fusion(bf16[1024,512]{1,0:T(8,128)(2,1)S(1)} %copy-done.2, f32[2048,512]{1,0:T(8,128)} %bitcast.74, f32[2048,512]{1,0:T(8,128)} %bitcast.73), kind=kOutput, calls=%fused_computation.6.clone.1 | convolution fusion | flops 2154823680 | bytes 11534336 | tf_op jit(solution)/shard_map/while/body/eval_jaxpr/dot_general | solution.py:103
  306.8 1.6 constant_dynamic-update-slice_fusion.2
  (86 shorter events, 2.6 us)
Async XLA Ops:
  6.5 151.9 %all-gather.3.cloned.1.call-start = ((), (), s32[]{:S(2)}) async-start(), calls=%async_computation | async-start | bytes 4210688 | tf_op jit(solution)/shard_map/all_gather | solution.py:80
  36.3 7.6 %copy-start.11 = (s32[64]{0:T(128)S(1)}, s32[64]{0:T(128)}, u32[]{:S(2)}) copy-start(s32[64]{0:T(128)} %param.11) | copy-start | bytes 772
  38.5 124.7 %collective-permute-start = (bf16[16,4096]{1,0:T(8,128)(2,1)S(1)}, bf16[16,4096]{1,0:T(8,128)(2,1)S(1)}, u32[]{:S(2)}, u32[]{:S(2)}) collective-permute-start(bf16[16,4096]{1,0:T(8,128)(2,1)S(1)} %slice.41), channel_id=1, source_target_pairs={{0,1},{1,2},{2,3},{3,4},{4,5},{5,6},{6,7},{7,8},{8,9},{9,10},{10,1... | collective-permute-start | bytes 393224 | tf_op jit(solution)/shard_map/ppermute | solution.py:20
  42.6 120.6 %collective-permute-start.1 = (bf16[16,4096]{1,0:T(8,128)(2,1)S(1)}, bf16[16,4096]{1,0:T(8,128)(2,1)S(1)}, u32[]{:S(2)}, u32[]{:S(2)}) collective-permute-start(bf16[16,4096]{1,0:T(8,128)(2,1)S(1)} %slice.43), channel_id=1, source_target_pairs={{1,0},{2,1},{3,2},{4,3},{5,4},{6,5},{7,6},{8,7},{9,8},{10,9},{11,1... | collective-permute-start | bytes 393224 | tf_op jit(solution)/shard_map/ppermute | solution.py:23
  133.2 2.9 copy-start.10
  133.2 2.9 copy-start.9
  133.2 3.0 copy-start.8
  163.8 1.0 copy-start.3
  164.9 1.0 copy-start
  166.8 1.3 copy-start.6
  173.1 6.9 %copy-start.4 = (bf16[64,4,512]{0,1,2:T(4,128)(2,1)S(1)}, bf16[64,4,512]{0,1,2:T(4,128)(2,1)}, u32[]{:S(2)}) copy-start(bf16[64,4,512]{0,1,2:T(4,128)(2,1)} %get-tuple-element.174) | copy-start | bytes 786436 | tf_op jit(solution)/shard_map/while
  180.0 1.3 copy-start.7
  186.2 6.9 %copy-start.2 = (bf16[1024,512]{1,0:T(8,128)(2,1)S(1)}, bf16[1024,512]{1,0:T(8,128)(2,1)}, u32[]{:S(2)}) copy-start(bf16[1024,512]{1,0:T(8,128)(2,1)} %get-tuple-element.163) | copy-start | bytes 3145732 | tf_op jit(solution)/shard_map/while
  199.0 1.6 copy-start.1
  199.0 1.8 copy-start.5
  200.8 1.0 copy-start
  202.7 1.3 copy-start.6
  209.0 6.9 %copy-start.4 = (bf16[64,4,512]{0,1,2:T(4,128)(2,1)S(1)}, bf16[64,4,512]{0,1,2:T(4,128)(2,1)}, u32[]{:S(2)}) copy-start(bf16[64,4,512]{0,1,2:T(4,128)(2,1)} %get-tuple-element.174) | copy-start | bytes 786436 | tf_op jit(solution)/shard_map/while
  215.9 1.3 copy-start.7
  222.2 6.9 %copy-start.2 = (bf16[1024,512]{1,0:T(8,128)(2,1)S(1)}, bf16[1024,512]{1,0:T(8,128)(2,1)}, u32[]{:S(2)}) copy-start(bf16[1024,512]{1,0:T(8,128)(2,1)} %get-tuple-element.163) | copy-start | bytes 3145732 | tf_op jit(solution)/shard_map/while
  234.9 1.6 copy-start.1
  234.9 1.8 copy-start.5
  236.8 1.0 copy-start
  238.7 1.3 copy-start.6
  245.0 6.9 %copy-start.4 = (bf16[64,4,512]{0,1,2:T(4,128)(2,1)S(1)}, bf16[64,4,512]{0,1,2:T(4,128)(2,1)}, u32[]{:S(2)}) copy-start(bf16[64,4,512]{0,1,2:T(4,128)(2,1)} %get-tuple-element.174) | copy-start | bytes 786436 | tf_op jit(solution)/shard_map/while
  251.9 1.3 copy-start.7
  258.1 6.9 %copy-start.2 = (bf16[1024,512]{1,0:T(8,128)(2,1)S(1)}, bf16[1024,512]{1,0:T(8,128)(2,1)}, u32[]{:S(2)}) copy-start(bf16[1024,512]{1,0:T(8,128)(2,1)} %get-tuple-element.163) | copy-start | bytes 3145732 | tf_op jit(solution)/shard_map/while
  270.9 1.6 copy-start.1
  270.9 1.8 copy-start.5
  272.7 1.0 copy-start
  274.6 1.3 copy-start.6
  280.9 6.9 %copy-start.4 = (bf16[64,4,512]{0,1,2:T(4,128)(2,1)S(1)}, bf16[64,4,512]{0,1,2:T(4,128)(2,1)}, u32[]{:S(2)}) copy-start(bf16[64,4,512]{0,1,2:T(4,128)(2,1)} %get-tuple-element.174) | copy-start | bytes 786436 | tf_op jit(solution)/shard_map/while
  287.8 1.3 copy-start.7
  294.1 6.9 %copy-start.2 = (bf16[1024,512]{1,0:T(8,128)(2,1)S(1)}, bf16[1024,512]{1,0:T(8,128)(2,1)}, u32[]{:S(2)}) copy-start(bf16[1024,512]{1,0:T(8,128)(2,1)} %get-tuple-element.163) | copy-start | bytes 3145732 | tf_op jit(solution)/shard_map/while
  306.8 1.6 copy-start.1
  306.8 1.8 copy-start.5
Sparse Core Ops, SparseCore 0:
  38.4 119.9 all-gather.2
where the time goes:
time: 316 us
  blocking collectives  88.9 us (28%)
  matrix products  80.2 us (25%)
  local copies, waits for them, and re-layouts  79.5 us (25%)
  other arithmetic  22.8 us (7%)
  between operations  21.9 us (7%)
  waiting for transfers between devices  16.6 us (5%)
  starting transfers between devices  5.32 us (2%)
    psum x1, blocking collectives, per_device(): references = lax.psum(selected, ('fibre', 'chan')).astype(jnp.bfloat16)  88.9 us
    add x4, local copies, waits for them, and re-layouts, correlate(): jnp.einsum('csf,rsf->crf', a_re, ref_re, preferred_element_type=jnp.float32)  27.7 us
    sub x4, local copies, waits for them, and re-layouts, correlate(): jnp.einsum('csf,rsf->crf', a_im, ref_re, preferred_element_type=jnp.float32)  27.7 us
    dot_general x4, matrix products, correlate(): jnp.dot(cross.reshape(group * REFS, SEG), kernel, preferred_element_type=...  23.2 us
    another operation x3, other arithmetic  20.4 us
    dot_general x4, matrix products, correlate(): jnp.einsum('csf,rsf->crf', a_re, ref_im, preferred_element_type=jnp.float32)  19.8 us
    dot_general x4, matrix products, correlate(): jnp.einsum('csf,rsf->crf', a_im, ref_im, preferred_element_type=jnp.float32)  19.8 us
    all_gather x1, waiting for transfers between devices, per_device(): piece = lax.all_gather(exported, ('fibre', 'chan'), axis=0, tiled=True)  16.6 us
  transfers between devices with their start and end apart: 3, of which 1 were waited for; matrix products, arithmetic and copies ran while one was open for 4% of the time, Pallas kernels for 0%

commit v1 on v0

--- a/solution.py
+++ b/solution.py
@@ -62,7 +62,7 @@
     columns = jnp.arange(local_ch, dtype=jnp.int32)
     pick = (ref_ids[:, None] - block_base == columns[None, :]).astype(jnp.bfloat16)
     selected = jnp.dot(pick, flat, preferred_element_type=jnp.float32)
-    references = lax.psum(selected, ("fibre", "chan")).astype(jnp.bfloat16)
+    references = lax.psum(lax.psum(selected, "fibre"), "chan").astype(jnp.bfloat16)
     extended = with_halo(flat, (("chan", 0),), HALO)
     ext_rows = local_ch + 2 * HALO
     position = near_ids - (block_base - HALO)

time: 316 us -> 928 us (2.94)
  the two profiles are of different devices: /device:TPU:1 before, /device:TPU:0 now
where the time goes in v1:
time: 928 us
  blocking collectives  696 us (75%)
  matrix products  81.2 us (9%)
  local copies, waits for them, and re-layouts  79.5 us (9%)
  between operations  23.4 us (3%)
  other arithmetic  22.8 us (2%)
  waiting for transfers between devices  21.4 us (2%)
    psum x1, blocking collectives, per_device(): lax.psum(lax.psum(selected, 'fibre'), 'chan').astype(jnp.bfloat16)  696 us
    add x4, local copies, waits for them, and re-layouts, correlate(): jnp.einsum('csf,rsf->crf', a_re, ref_re, preferred_element_type=jnp.float32)  27.7 us
    sub x4, local copies, waits for them, and re-layouts, correlate(): jnp.einsum('csf,rsf->crf', a_im, ref_re, preferred_element_type=jnp.float32)  27.7 us
    dot_general x4, matrix products, correlate(): jnp.dot(cross.reshape(group * REFS, SEG), kernel, preferred_element_type=...  23.2 us
    psum x1, waiting for transfers between devices, per_device(): lax.psum(selected, 'fibre')  21.4 us
    another operation x3, other arithmetic  20.4 us
    dot_general x4, matrix products, correlate(): jnp.einsum('csf,rsf->crf', a_re, ref_im, preferred_element_type=jnp.float32)  19.8 us
    dot_general x4, matrix products, correlate(): jnp.einsum('csf,rsf->crf', a_im, ref_im, preferred_element_type=jnp.float32)  19.8 us
  transfers between devices with their start and end apart: 4, of which 1 were waited for; matrix products, arithmetic and copies ran while one was open for 2% of the time, Pallas kernels for 0%

profile of v1, /device:TPU:0, one launch (start us, length us, event | category | flops | bytes accessed | tf_op | source)
XLA Modules:
  0.0 927.5 jit_solution(11350927454836523799)
XLA Ops:
  7.4 1.5 fusion.53
  13.9 8.0 negate_convert_fusion
  24.4 1.9 dynamic-slice_bitcast_fusion.3
  26.4 0.8 copy.42
  27.3 0.3 reshape.58
  27.6 7.9 multiply_convert_fusion
  35.5 1.3 multiply_reduce_fusion
  36.9 0.3 divide_convert_fusion
  37.2 0.7 reshape.59
  37.9 1.4 fusion.45
  40.0 0.6 fusion.46
  40.8 1.8 collective-permute-start
  42.7 1.3 collective-permute-start.1
  44.3 4.5 multiply_convert_fusion.2
  48.8 1.0 pad_maximum_fusion.1
  49.8 21.4 %all-reduce.3.cloned.1.call-done = f32[64,4096]{1,0:T(8,128)} async-done(((f32[64,4096]{1,0:T(8,128)}), f32[64,4096]{1,0:T(8,128)}) %all-reduce.3.cloned.1.call-update) | async-done | bytes 1048592 | tf_op jit(solution)/shard_map/psum | solution.py:65
  71.2 695.8 %all-reduce.4 = bf16[64,4096]{1,0:T(8,128)(2,1)S(1)} all-reduce(f32[64,4096]{1,0:T(8,128)} %all-reduce.3.cloned.1.call-done), channel_id=1, replica_groups=mesh['fibre'=2,'chan'=128] {'chan'}, use_global_device_ids=true, to_apply=%region_5.6 | all-reduce | flops 262144 | bytes 1572864 | tf_op jit(solution)/shard_map/psum | solution.py:65
  767.0 0.4 reshape.61
  767.6 1.1 copy.48
  768.7 1.1 copy.49
  769.8 4.7 fusion.25
  774.6 0.6 fusion.17
  775.2 0.8 reshape.60
  776.2 143.8 %while.11 = (s32[]{:T(128)}, bf16[4,32,64,512]{3,2,1,0:T(8,128)(2,1)}, bf16[4,32,4,1024]{3,2,1,0:T(4,128)(2,1)S(1)}, bf16[64,4,512]{0,1,2:T(4,128)(2,1)S(1)}, bf...) while((s32[]{:T(128)}, ...), condition=%wide.region_7.8_spmd, body=%wide.region_6.7_spmd.sunk | while | flops 2190475264 | bytes 77595424 | solution.py:106
  776.3 1.0 copy-done
  777.4 0.8 copy.57
  778.2 1.3 fusion.87
  779.5 4.9 add_bitcast_fusion.2
  784.4 6.9 copy.59
  791.3 1.3 fusion.86
  792.7 4.9 subtract_bitcast_fusion.2
  797.6 6.9 copy.58
  804.5 5.8 fusion.88
  810.4 1.6 constant_dynamic-update-slice_fusion.2
  812.2 1.0 copy-done
  813.3 0.8 copy.57
  814.1 1.3 fusion.87
  815.4 4.9 add_bitcast_fusion.2
  820.4 6.9 copy.59
  827.3 1.3 fusion.86
  828.6 4.9 subtract_bitcast_fusion.2
  833.6 6.9 copy.58
  840.5 5.8 fusion.88
  846.3 1.6 constant_dynamic-update-slice_fusion.2
  848.2 1.0 copy-done
  849.3 0.8 copy.57
  850.1 1.3 fusion.87
  851.4 4.9 add_bitcast_fusion.2
  856.3 6.9 copy.59
  863.3 1.3 fusion.86
  864.6 4.9 subtract_bitcast_fusion.2
  869.5 6.9 copy.58
  876.4 5.8 fusion.88
  882.3 1.6 constant_dynamic-update-slice_fusion.2
  884.1 1.0 copy-done
  885.2 0.8 copy.57
  886.0 1.3 fusion.87
  887.3 4.9 add_bitcast_fusion.2
  892.3 6.9 copy.59
  899.2 1.3 fusion.86
  900.5 4.9 subtract_bitcast_fusion.2
  905.5 6.9 copy.58
  912.4 5.8 fusion.88
  918.2 1.6 constant_dynamic-update-slice_fusion.2
  (89 shorter events, 2.7 us)
Async XLA Ops:
  7.4 63.8 %all-reduce.3.cloned.1.call-start = ((), (), s32[]{:S(2)}) async-start(), calls=%async_computation | async-start | bytes 2097152 | tf_op jit(solution)/shard_map/psum | solution.py:65
  36.9 1.0 copy-start.11
  37.9 6.1 copy-start.10
  37.9 6.1 copy-start.9
  37.9 6.3 copy-start.8
  39.3 730.6 %all-gather.3.cloned.1.call-start = ((), (), s32[]{:S(2)}) async-start(), calls=%async_computation.1 | async-start | bytes 4210688 | tf_op jit(solution)/shard_map/all_gather | solution.py:80
  40.8 733.8 %collective-permute-start = (bf16[16,4096]{1,0:T(8,128)(2,1)S(1)}, bf16[16,4096]{1,0:T(8,128)(2,1)S(1)}, u32[]{:S(2)}, u32[]{:S(2)}) collective-permute-start(bf16[16,4096]{1,0:T(8,128)(2,1)S(1)} %slice.41), channel_id=1, source_target_pairs={{0,1},{1,2},{2,3},{3,4},{4,5},{5,6},{6,7},{7,8},{8,9},{9,10},{10,1... | collective-permute-start | bytes 393224 | tf_op jit(solution)/shard_map/ppermute | solution.py:20
  42.7 731.9 %collective-permute-start.1 = (bf16[16,4096]{1,0:T(8,128)(2,1)S(1)}, bf16[16,4096]{1,0:T(8,128)(2,1)S(1)}, u32[]{:S(2)}, u32[]{:S(2)}) collective-permute-start(bf16[16,4096]{1,0:T(8,128)(2,1)S(1)} %slice.43), channel_id=1, source_target_pairs={{1,0},{2,1},{3,2},{4,3},{5,4},{6,5},{7,6},{8,7},{9,8},{10,9},{11,1... | collective-permute-start | bytes 393224 | tf_op jit(solution)/shard_map/ppermute | solution.py:23
  775.2 1.0 copy-start.3
  776.2 1.0 copy-start
  778.1 1.3 copy-start.6
  784.4 6.9 copy-start.4
  791.3 1.3 copy-start.7
  797.6 6.9 copy-start.2
  810.4 1.6 copy-start.1
  810.4 1.8 copy-start.5
  812.2 1.0 copy-start
  814.1 1.3 copy-start.6
  820.4 6.9 copy-start.4
  827.3 1.3 copy-start.7
  833.6 6.9 copy-start.2
  846.3 1.6 copy-start.1
  846.3 1.8 copy-start.5
  848.2 1.0 copy-start
  850.1 1.3 copy-start.6
  856.3 6.9 copy-start.4
  863.3 1.3 copy-start.7
  869.5 6.9 copy-start.2
  882.3 1.6 copy-start.1
  882.3 1.8 copy-start.5
  884.1 1.0 copy-start
  886.0 1.3 copy-start.6
  892.3 6.9 copy-start.4
  899.2 1.3 copy-start.7
  905.5 6.9 copy-start.2
  918.2 1.6 copy-start.1
  918.2 1.8 copy-start.5
Sparse Core Ops, SparseCore 0:
  39.4 31.7 all-reduce.2
Sparse Core Ops, SparseCore 1:
  43.5 117.2 all-gather.2
